TPU v7x, 256 devices: a whole 4x4x8 slice. The times are simulated.
256 devices in a mesh: row: 32 (over x, y, z_lo), src: 8 (over z_hi, core).
Axes of the slice: x: 4, y: 4, z: 8 (z_hi: 4, z_lo: 2; z = z_hi * 2 + z_lo), core: 2. Of those that a mesh axis runs over, the one named last changes fastest.
Arguments:
- traces: bfloat16 [16384, 128, 512], P('row', 'src'), may hold values from -6 to 6
- row_source: int32 [16384], P('row'), may hold values from 0 to 16383, as said below
- slice_data: bfloat16 [2, 16384, 32, 512], P(None, 'row', None, 'src'), may hold values from -0.03125 to 0.03125
- wavelet_inverse: float32 [2], replicated, may hold values from 0.3 to 0.8
Outputs:
- multiples: float32 [16384, 2, 128], P(('row', 'src'))
- primaries: float32 [16384, 2, 128], P(('row', 'src'))
Inputs may be any that keep to these rules, and one draw needn't show every extreme that they name: `row_source`: every recording row is named exactly once; entry e * 512 + p names a recording row whose index modulo 512 lies in [e * 16, (e + 1) * 16).
All inputs are finite; a program needn't handle non-finite values.
Results may differ from a plain program's by a relative error of at most 0.0056.
Values may be sent and summed in bfloat16 or wider, within the bound.
A program may use at most 64 MiB of HBM per device.

v0:
```python
import jax
import jax.numpy as jnp
from jax import lax
from jax.sharding import PartitionSpec as P

FREQ = 61
ITERS = 3


def dft_kernel(samples):
    ticks = jnp.arange(samples, dtype=jnp.int32)
    moment = ticks.astype(jnp.float32)
    ramp_len = samples // 8
    rising = 0.5 - 0.5 * jnp.cos(jnp.pi * (moment + 0.5) / ramp_len)
    falling = 0.5 - 0.5 * jnp.cos(jnp.pi * (samples - moment - 0.5) / ramp_len)
    taper = jnp.where(
        ticks < ramp_len,
        rising,
        jnp.where(ticks >= samples - ramp_len, falling, jnp.ones_like(rising)),
    )
    wrapped = ticks * FREQ % samples
    angles = 2.0 * jnp.pi / samples * wrapped.astype(jnp.float32)
    factor = 1.0 / jnp.sqrt(jnp.float32(samples))
    table = jnp.stack([taper * jnp.cos(angles) * factor, -taper * jnp.sin(angles) * factor], axis=1)
    return table.astype(jnp.bfloat16)


def combine_parts(real_terms, imag_terms, shot_count):
    pred_real = real_terms[:, :shot_count] - imag_terms[:, shot_count:]
    pred_imag = real_terms[:, shot_count:] + imag_terms[:, :shot_count]
    return jnp.stack([pred_real, pred_imag], axis=1)


def body(traces, row_source, slice_data, wavelet_inverse):
    block_rows, shot_local, samples = traces.shape
    kernel = dft_kernel(samples)
    spectra = jnp.dot(
        traces.reshape(block_rows * shot_local, samples), kernel, preferred_element_type=jnp.float32
    )
    spectra = jnp.transpose(spectra.reshape(block_rows, shot_local, 2), (0, 2, 1)).astype(
        jnp.bfloat16
    )
    arrived = lax.all_to_all(spectra, "row", split_axis=0, concat_axis=0, tiled=True)
    group_rows = block_rows // lax.axis_size("row")
    located = row_source // block_rows * group_rows + row_source % group_rows
    ordered = arrived[located]
    slice_rows = block_rows // lax.axis_size("src")
    panel = lax.all_to_all(ordered, "src", split_axis=0, concat_axis=2, tiled=True)
    shot_count = panel.shape[2]
    base = panel.astype(jnp.float32)
    wave_real = wavelet_inverse[0]
    wave_imag = wavelet_inverse[1]
    real_data = slice_data[0].reshape(block_rows, -1)
    imag_data = slice_data[1].reshape(block_rows, -1)
    estimate = panel
    predicted = jnp.zeros((slice_rows, 2, shot_count), jnp.float32)
    primaries = base
    for iteration in range(ITERS):
        shard_rows = lax.all_gather(estimate, "row", axis=0, tiled=True)
        piece_rows = shard_rows.shape[0]
        stacked = shard_rows.reshape(piece_rows, 2 * shot_count)
        real_terms = jnp.dot(real_data, stacked, preferred_element_type=jnp.float32)
        imag_terms = jnp.dot(imag_data, stacked, preferred_element_type=jnp.float32)
        summed = lax.psum(combine_parts(real_terms, imag_terms, shot_count), "src")
        predicted = lax.dynamic_slice_in_dim(
            summed, lax.axis_index("src") * slice_rows, slice_rows, 0
        )
        next_real = base[:, 0] - (wave_real * predicted[:, 0] - wave_imag * predicted[:, 1])
        next_imag = base[:, 1] - (wave_real * predicted[:, 1] + wave_imag * predicted[:, 0])
        primaries = jnp.stack([next_real, next_imag], axis=1)
        estimate = primaries.astype(jnp.bfloat16)
    return (predicted, primaries)


def solution(mesh):
    in_specs = (P("row", "src", None), P("row"), P(None, "row", None, "src"), P())
    out_specs = (P(("row", "src"), None, None), P(("row", "src"), None, None))
    return jax.shard_map(body, mesh=mesh, in_specs=in_specs, out_specs=out_specs, check_vma=False)
```

profile of v0, /device:TPU:1, one launch (start us, length us, event | category | flops | bytes accessed | tf_op | source)
XLA Modules:
  0.0 753.6 jit_solution(3112653908474504425)
XLA Ops:
  7.2 0.1 multiply_convert_fusion
  7.3 5.6 fusion
  12.9 0.2 convert_element_type.54
  13.2 0.3 copy.48
  13.5 0.9 reshape.153
  14.3 9.2 %all-to-all-start = ((bf16[32,2,256]{2,1,0:T(2,128)(2,1)}), bf16[32,2,256]{2,1,0:T(2,128)(2,1)S(1)}, u32[]{:S(2)}, u32[]{:S(2)}) async-start(bf16[32,2,256]{2,1,0:T(2,128)(2,1)} %reshape.153), calls=%async_computation | async-start | bytes 65536 | tf_op jit(solution)/shard_map/all_to_all | solution.py:43
  23.5 0.0 all-gather.4.cloned.1.call-start
  23.6 7.0 all-to-all-done
  30.7 0.2 reshape.154
  30.9 2.1 gather_fusion
  33.0 0.3 reshape.155
  33.3 16.6 %all_to_all.23 = bf16[8,2,1024]{2,1,0:T(2,128)(2,1)S(1)} all-to-all(bf16[8,2,1024]{2,1,0:T(2,128)(2,1)S(1)} %reshape.155), channel_id=1, replica_groups=mesh['row'=32,'src'=8] {'src'}, dimensions={0} | all-to-all | bytes 65536 | tf_op jit(solution)/shard_map/all_to_all | solution.py:48
  49.9 0.2 reshape.156
  50.1 0.2 copy.14
  50.3 0.7 copy.15
  51.0 0.0 all-reduce.4.cloned.1.call-start
  51.1 4.0 fusion.41
  55.0 120.7 %all-gather.4.cloned.1.call-done = bf16[2048,2,128]{2,1,0:T(2,128)(2,1)} async-done(((bf16[64,2,128]{2,1,0:T(2,128)(2,1)}), bf16[2048,2,128]{2,1,0:T(2,128)(2,1)}) %all-gather.4.cloned.1.call-update) | async-done | bytes 1048592 | tf_op jit(solution)/shard_map/all_gather | solution.py:59
  175.7 2.7 convolution_bitcast_fusion.4
  178.4 0.7 convolution_bitcast_fusion.5
  179.2 0.1 fusion.18
  179.3 0.8 pad_maximum_fusion
  180.1 0.0 all-gather.6.cloned.1.call-start
  180.2 0.6 fusion.42
  180.8 94.4 %all-reduce.4.cloned.1.call-done = f32[512,2,128]{0,2,1:T(8,128)} async-done(((f32[512,2,128]{0,2,1:T(8,128)}), f32[512,2,128]{0,2,1:T(8,128)}) %all-reduce.4.cloned.1.call-update) | async-done | bytes 524304 | tf_op jit(solution)/shard_map/psum | solution.py:64
  275.3 2.1 subtract_convert_fusion.3
  277.4 0.7 copy.16
  278.2 0.0 all-reduce.6.cloned.1.call-start
  278.2 131.0 %all-gather.6.cloned.1.call-done = bf16[2048,2,128]{2,1,0:T(2,128)(2,1)} async-done(((bf16[64,2,128]{2,1,0:T(2,128)(2,1)}), bf16[2048,2,128]{2,1,0:T(2,128)(2,1)}) %all-gather.6.cloned.1.call-update) | async-done | bytes 1048592 | tf_op jit(solution)/shard_map/all_gather | solution.py:59
  409.2 2.7 convolution_bitcast_fusion.2
  411.9 0.7 convolution_bitcast_fusion.3
  412.7 0.1 fusion.16
  412.8 0.8 pad_maximum_fusion.1
  413.6 0.0 all-gather.8.cloned.1.call-start
  413.7 95.0 %all-reduce.6.cloned.1.call-done = f32[512,2,128]{0,2,1:T(8,128)} async-done(((f32[512,2,128]{0,2,1:T(8,128)}), f32[512,2,128]{0,2,1:T(8,128)}) %all-reduce.6.cloned.1.call-update) | async-done | bytes 524304 | tf_op jit(solution)/shard_map/psum | solution.py:64
  508.6 2.1 subtract_convert_fusion.1
  510.8 0.7 copy.17
  511.6 0.0 all-reduce.8.cloned.1.call-start
  511.6 131.0 %all-gather.8.cloned.1.call-done = bf16[2048,2,128]{2,1,0:T(2,128)(2,1)} async-done(((bf16[64,2,128]{2,1,0:T(2,128)(2,1)}), bf16[2048,2,128]{2,1,0:T(2,128)(2,1)}) %all-gather.8.cloned.1.call-update) | async-done | bytes 1048592 | tf_op jit(solution)/shard_map/all_gather | solution.py:59
  642.6 2.7 convolution_bitcast_fusion
  645.3 0.7 convolution_bitcast_fusion.1
  646.0 0.1 fusion.14
  646.1 0.8 pad_maximum_fusion.2
  647.0 95.1 %all-reduce.8.cloned.1.call-done = f32[512,2,128]{0,2,1:T(8,128)} async-done(((f32[512,2,128]{0,2,1:T(8,128)}), f32[512,2,128]{0,2,1:T(8,128)}) %all-reduce.8.cloned.1.call-update) | async-done | bytes 524304 | tf_op jit(solution)/shard_map/psum | solution.py:64
  742.1 1.0 constant_dynamic-slice_fusion
  743.1 0.7 copy.18
  743.8 2.1 subtract_subtract_fusion
  746.0 0.7 copy.19
  (22 shorter events, 0.2 us)
Async XLA Ops:
  7.3 16.3 %copy-start = (s32[512]{0:T(512)S(1)}, s32[512]{0:T(512)}, u32[]{:S(2)}) copy-start(s32[512]{0:T(512)} %param.5) | copy-start | bytes 6148
  14.3 16.3 %all-to-all-start = ((bf16[32,2,256]{2,1,0:T(2,128)(2,1)}), bf16[32,2,256]{2,1,0:T(2,128)(2,1)S(1)}, u32[]{:S(2)}, u32[]{:S(2)}) async-start(bf16[32,2,256]{2,1,0:T(2,128)(2,1)} %reshape.153), calls=%async_computation | async-start | bytes 65536 | tf_op jit(solution)/shard_map/all_to_all | solution.py:43
  23.5 152.2 %all-gather.4.cloned.1.call-start = ((), (), s32[]{:S(2)}) async-start(), calls=%async_computation.2 | async-start | bytes 1081344 | tf_op jit(solution)/shard_map/all_gather | solution.py:59
  51.0 224.2 %all-reduce.4.cloned.1.call-start = ((), (), s32[]{:S(2)}) async-start(), calls=%async_computation.3 | async-start | bytes 1048576 | tf_op jit(solution)/shard_map/psum | solution.py:64
  175.7 2.7 copy-start.2
  179.2 1.0 copy-start.1
  180.1 229.1 %all-gather.6.cloned.1.call-start = ((), (), s32[]{:S(2)}) async-start(), calls=%async_computation.4 | async-start | bytes 1081344 | tf_op jit(solution)/shard_map/all_gather | solution.py:59
  278.2 230.5 %all-reduce.6.cloned.1.call-start = ((), (), s32[]{:S(2)}) async-start(), calls=%async_computation.5 | async-start | bytes 1048576 | tf_op jit(solution)/shard_map/psum | solution.py:64
  409.2 2.7 copy-start.4
  413.6 228.9 %all-gather.8.cloned.1.call-start = ((), (), s32[]{:S(2)}) async-start(), calls=%async_computation.6 | async-start | bytes 1081344 | tf_op jit(solution)/shard_map/all_gather | solution.py:59
  511.6 230.6 %all-reduce.8.cloned.1.call-start = ((), (), s32[]{:S(2)}) async-start(), calls=%async_computation.7 | async-start | bytes 1048576 | tf_op jit(solution)/shard_map/psum | solution.py:64
  642.6 2.7 copy-start.3
Sparse Core Ops, SparseCore 0:
  51.1 124.5 all-gather.3
  180.3 94.9 all-reduce.3
  278.3 130.8 all-gather.5
  413.7 94.8 all-reduce.5
  511.7 130.8 all-gather.7
  647.1 94.9 all-reduce.7
where the time goes:
time: 754 us
  waiting for transfers between devices  674 us (89%)
  blocking collectives  16.6 us (2%)
  matrix products  16 us (2%)
  between operations  14.4 us (2%)
  local copies, waits for them, and re-layouts  13.5 us (2%)
  starting transfers between devices  9.46 us (1%)
  other arithmetic  9.38 us (1%)
    all_gather x3, waiting for transfers between devices, body(): shard_rows = lax.all_gather(estimate, 'row', axis=0, tiled=True)  383 us
    psum x3, waiting for transfers between devices, body(): summed = lax.psum(combine_parts(real_terms, imag_terms, shot_count), 'src')  285 us
    all_to_all x1, blocking collectives, body(): lax.all_to_all(ordered, 'src', split_axis=0, concat_axis=2, tiled=True)  16.6 us
  transfers between devices with their start and end apart: 7, of which 7 were waited for; matrix products, arithmetic and copies ran while one was open for 1% of the time, Pallas kernels for 0%

commit v1 on v0

v1 whole, which is shorter than its diff:
```python
import functools

import jax
import jax.numpy as jnp
from jax import lax
from jax.experimental import pallas as pl
from jax.experimental.pallas import tpu as pltpu
from jax.sharding import PartitionSpec as P

FREQ = 61
ITERS = 3
MESH = pl.DeviceIdType.MESH


def dft_kernel(samples):
    ticks = jnp.arange(samples, dtype=jnp.int32)
    moment = ticks.astype(jnp.float32)
    ramp_len = samples // 8
    rising = 0.5 - 0.5 * jnp.cos(jnp.pi * (moment + 0.5) / ramp_len)
    falling = 0.5 - 0.5 * jnp.cos(jnp.pi * (samples - moment - 0.5) / ramp_len)
    taper = jnp.where(
        ticks < ramp_len,
        rising,
        jnp.where(ticks >= samples - ramp_len, falling, jnp.ones_like(rising)),
    )
    wrapped = ticks * FREQ % samples
    angles = 2.0 * jnp.pi / samples * wrapped.astype(jnp.float32)
    factor = 1.0 / jnp.sqrt(jnp.float32(samples))
    table = jnp.stack([taper * jnp.cos(angles) * factor, -taper * jnp.sin(angles) * factor], axis=1)
    return table.astype(jnp.bfloat16)


def predict(n_row, n_zed, rows, lanes, wave_ref, panel_ref, data_ref, mult_ref, prim_ref,
            gathered, matrix, staged, part, mine, swapped, sent, came,
            load_sem, ag_send, ag_recv, sw_send, sw_recv, rs_send, rs_recv):
    row, src = lax.axis_index("row"), lax.axis_index("src")
    zed, core = lax.div(src, 2), lax.rem(src, 2)
    half = lanes // 2
    depth = n_row * rows

    barrier = pltpu.get_barrier_semaphore()

    @pl.loop(1, n_row)
    def _(k):
        pl.semaphore_signal(barrier, inc=1, device_id=(lax.rem(row + k, n_row), src), device_id_type=MESH)

    pl.semaphore_signal(barrier, inc=1, device_id=(row, zed * 2 + 1 - core), device_id_type=MESH)
    for k in range(1, n_zed):
        pl.semaphore_signal(
            barrier, inc=1, device_id=(row, lax.rem(zed + k, n_zed) * 2 + core), device_id_type=MESH
        )
    load = pltpu.make_async_copy(data_ref, staged, load_sem)
    load.start()
    pl.semaphore_wait(barrier, n_row - 1 + 1 + n_zed - 1)

    def send_block(it, k):
        return pltpu.make_async_remote_copy(
            src_ref=gathered.at[it, row],
            dst_ref=gathered.at[it, row],
            send_sem=ag_send.at[it],
            recv_sem=ag_recv.at[it],
            device_id=(lax.rem(row + k, n_row), src),
            device_id_type=MESH,
        )

    def all_but_one(ref):
        return ref.at[pl.ds(0, n_row - 1)]

    gathered[0, row] = panel_ref[...]

    @pl.loop(1, n_row)
    def _(k):
        send_block(0, k).start()

    load.wait()

    @pl.loop(0, 2)
    def _(c):
        @pl.loop(0, depth // 256)
        def _(k):
            at = pl.multiple_of(k * 256, 256)
            turned = staged[c, pl.ds(at, 256), :].T
            for z in range(n_zed):
                matrix[z, c, :, pl.ds(at, 256)] = turned[z * 2 * rows : (z + 1) * 2 * rows, :]

    wave_real, wave_imag = wave_ref[0], wave_ref[1]

    @pl.loop(0, ITERS)
    def _(it):
        pltpu.make_async_copy(all_but_one(gathered.at[it]), all_but_one(gathered.at[it]), ag_recv.at[it]).wait()
        estimate = gathered.at[it].reshape(depth, lanes)

        def swap(step):
            target = lax.rem(zed + step, n_zed)
            return pltpu.make_async_remote_copy(
                src_ref=part.at[it, target, 1 - core],
                dst_ref=swapped.at[it, target],
                send_sem=sw_send.at[it, step],
                recv_sem=sw_recv.at[it, step],
                device_id=(row, zed * 2 + 1 - core),
                device_id_type=MESH,
            )

        def scatter(step):
            target = lax.rem(zed + step, n_zed)
            return pltpu.make_async_remote_copy(
                src_ref=sent.at[it, step],
                dst_ref=came.at[it, step],
                send_sem=rs_send.at[it, step],
                recv_sem=rs_recv.at[it, step],
                device_id=(row, target * 2 + core),
                device_id_type=MESH,
            )

        order = [k for k in (2, 1, 3, 0) if k < n_zed]
        for step in order:
            target = lax.rem(zed + step, n_zed)
            left = matrix.at[target].reshape(2 * 2 * rows, depth)[...]
            terms = jnp.dot(left, estimate[...], preferred_element_type=jnp.float32)
            real_terms, imag_terms = terms[: 2 * rows], terms[2 * rows :]
            real = real_terms[:, :half] - imag_terms[:, half:]
            imag = real_terms[:, half:] + imag_terms[:, :half]
            for c in range(2):
                part[it, target, c, :, :half] = real[c * rows : (c + 1) * rows]
                part[it, target, c, :, half:] = imag[c * rows : (c + 1) * rows]
            swap(step).start()
        for step in order:
            swap(step).wait_recv()
            target = lax.rem(zed + step, n_zed)
            both = part[it, target, core] + swapped[it, target]
            if step:
                sent[it, step] = both.astype(jnp.bfloat16)
                scatter(step).start()
            else:
                mine[...] = both
        total = mine[...]
        for step in order[:-1]:
            scatter(step).wait_recv()
            total = total + came[it, step].astype(jnp.float32)
        real, imag = total[:, :half], total[:, half:]
        base = panel_ref[...].astype(jnp.float32)
        next_real = base[:, :half] - (wave_real * real - wave_imag * imag)
        next_imag = base[:, half:] - (wave_real * imag + wave_imag * real)
        mult_ref[...] = total
        prim_ref[:, :half] = next_real
        prim_ref[:, half:] = next_imag

        @pl.when(it + 1 < ITERS)
        def _():
            gathered[it + 1, row, :, :half] = next_real.astype(jnp.bfloat16)
            gathered[it + 1, row, :, half:] = next_imag.astype(jnp.bfloat16)

            @pl.loop(1, n_row)
            def _(k):
                send_block(it + 1, k).start()

        pltpu.make_async_copy(all_but_one(gathered.at[it]), all_but_one(gathered.at[it]), ag_send.at[it]).wait()
        for step in order:
            swap(step).wait_send()
            if step:
                scatter(step).wait_send()


def body(traces, row_source, slice_data, wavelet_inverse):
    block_rows, shot_local, samples = traces.shape
    n_row, n_src = lax.axis_size("row"), lax.axis_size("src")
    n_zed = n_src // 2
    kernel = dft_kernel(samples)
    spectra = jnp.dot(
        traces.reshape(block_rows * shot_local, samples), kernel, preferred_element_type=jnp.float32
    )
    spectra = jnp.transpose(spectra.reshape(block_rows, shot_local, 2), (0, 2, 1)).astype(
        jnp.bfloat16
    )
    arrived = lax.all_to_all(spectra, "row", split_axis=0, concat_axis=0, tiled=True)
    group_rows = block_rows // n_row
    located = row_source // block_rows * group_rows + row_source % group_rows
    ordered = arrived[located]
    slice_rows = block_rows // n_src
    panel = lax.all_to_all(ordered, "src", split_axis=0, concat_axis=2, tiled=True)
    shot_count = panel.shape[2]
    lanes = 2 * shot_count
    panel = panel.reshape(slice_rows, lanes)
    depth = n_row * slice_rows
    data = jnp.transpose(slice_data, (0, 2, 3, 1)).reshape(2, depth, block_rows)
    f32, bf16 = jnp.float32, jnp.bfloat16
    block = jax.ShapeDtypeStruct((slice_rows, lanes), f32)
    sems = pltpu.SemaphoreType.DMA
    multiples, primaries = pl.pallas_call(
        functools.partial(predict, n_row, n_zed, slice_rows, lanes),
        out_shape=(block, block),
        in_specs=[
            pl.BlockSpec(memory_space=pltpu.SMEM),
            pl.BlockSpec(memory_space=pltpu.VMEM),
            pl.BlockSpec(memory_space=pl.ANY),
        ],
        out_specs=(pl.BlockSpec(memory_space=pltpu.VMEM),) * 2,
        scratch_shapes=[
            pltpu.VMEM((ITERS, n_row, slice_rows, lanes), bf16),
            pltpu.VMEM((n_zed, 2, 2 * slice_rows, depth), bf16),
            pltpu.VMEM((2, depth, block_rows), bf16),
            pltpu.VMEM((ITERS, n_zed, 2, slice_rows, lanes), f32),
            pltpu.VMEM((slice_rows, lanes), f32),
            pltpu.VMEM((ITERS, n_zed, slice_rows, lanes), f32),
            pltpu.VMEM((ITERS, n_zed, slice_rows, lanes), bf16),
            pltpu.VMEM((ITERS, n_zed, slice_rows, lanes), bf16),
            sems,
            sems((ITERS,)),
            sems((ITERS,)),
            sems((ITERS, n_zed)),
            sems((ITERS, n_zed)),
            sems((ITERS, n_zed)),
            sems((ITERS, n_zed)),
        ],
        compiler_params=pltpu.CompilerParams(
            collective_id=0, has_side_effects=True, vmem_limit_bytes=48 << 20
        ),
        name="predict",
    )(wavelet_inverse, panel, data)
    shape = (slice_rows, 2, shot_count)
    return multiples.reshape(shape), primaries.reshape(shape)


def solution(mesh):
    in_specs = (P("row", "src", None), P("row"), P(None, "row", None, "src"), P())
    out_specs = (P(("row", "src"), None, None), P(("row", "src"), None, None))
    return jax.shard_map(body, mesh=mesh, in_specs=in_specs, out_specs=out_specs, check_vma=False)
```

time: 754 us -> 119 us (0.16)
  waiting for transfers between devices: 674 us -> 7.09 us
  Pallas kernels: 0 us -> 69.7 us
  between operations: 14.4 us -> 0.75 us
  matrix products: 16 us -> 5.65 us
  other arithmetic: 9.38 us -> 0.14 us
    all_gather x3 -> x0, waiting for transfers between devices: 383 us -> none  [body(): shard_rows = lax.all_gather(estimate, 'row', axis=0, tiled=True)]
    psum x3 -> x0, waiting for transfers between devices: 285 us -> none  [body(): summed = lax.psum(combine_parts(real_terms, imag_terms, shot_count), 'src')]
    pallas_call x0 -> x1, Pallas kernels: none -> 69.7 us  [body(): pl.pallas_call(functools.partial(predict, n_row, n_zed, slice_rows, lanes...]
    dot_general x6 -> x0, matrix products: 10.4 us -> none  [the longest x3 8.18 us: body(): imag_terms = jnp.dot(imag_data, stacked, preferred_element_type=jnp.float32)]
  transfers between devices with their start and end apart: 7 -> 1, of which waited for: 7 -> 1; matrix products, arithmetic and copies ran while one was open for 1% -> 0% of each run, Pallas kernels for 0% -> 0%
where the time goes in v1:
time: 119 us; the launch traced here: 117 us
  Pallas kernels  69.7 us (59%)
  blocking collectives  16.6 us (14%)
  starting transfers between devices  9.21 us (8%)
  local copies, waits for them, and re-layouts  7.96 us (7%)
  waiting for transfers between devices  7.09 us (6%)
  matrix products  5.65 us (5%)
    pallas_call x1, Pallas kernels, body(): pl.pallas_call(functools.partial(predict, n_row, n_zed, slice_rows, lanes...  69.7 us
    all_to_all x1, blocking collectives, body(): lax.all_to_all(ordered, 'src', split_axis=0, concat_axis=2, tiled=True)  16.6 us
    all_to_all x1, starting transfers between devices, body(): lax.all_to_all(spectra, 'row', split_axis=0, concat_axis=0, tiled=True)  9.21 us
    all_to_all x1, waiting for transfers between devices, body(): lax.all_to_all(spectra, 'row', split_axis=0, concat_axis=0, tiled=True)  7.09 us
    dot_general x1, matrix products, body(): jnp.dot(traces.reshape(block_rows * shot_local, samples), kernel, preferr...  5.65 us
    unnamed x10, local copies, waits for them, and re-layouts  3.76 us
  transfers between devices with their start and end apart: 1, of which 1 were waited for; matrix products, arithmetic and copies ran while one was open for 0% of the time, Pallas kernels for 0%

profile of v1, /device:TPU:1, one launch (start us, length us, event | category | flops | bytes accessed | tf_op | source)
XLA Modules:
  0.0 117.1 jit_solution(10424728209600003088)
XLA Ops:
  0.6 0.0 copy-start.2
  0.6 0.0 copy-start.1
  0.6 0.1 multiply_convert_fusion
  0.8 5.6 %fusion = bf16[8192,2]{0,1:T(2,128)(2,1)S(1)} fusion(bf16[8192,512]{1,0:T(8,128)(2,1)} %bitcast.18, bf16[512,1]{0,1:T(2,128)(2,1)S(1)} %get-tuple-element.6, bf16[512,1]{0,1:T(2,128)(2,1)S(1)} %get-tuple-element.7), kind=kOutput, calls=%fused_computation.2 | convolution fusion | flops 16797696 | bytes 8423424 | tf_op jit(solution)/shard_map/dot_general | solution.py:169
  6.4 0.2 convert_element_type.49
  6.7 0.3 copy.17
  6.9 0.9 reshape.158
  7.8 9.2 %all-to-all-start = ((bf16[32,2,256]{2,1,0:T(2,128)(2,1)}), bf16[32,2,256]{2,1,0:T(2,128)(2,1)S(1)}, u32[]{:S(2)}, u32[]{:S(2)}) async-start(bf16[32,2,256]{2,1,0:T(2,128)(2,1)} %reshape.158), calls=%async_computation | async-start | bytes 65536 | tf_op jit(solution)/shard_map/all_to_all | solution.py:175
  17.0 0.0 copy-done.2
  17.1 7.1 %all-to-all-done = bf16[32,2,256]{2,1,0:T(2,128)(2,1)S(1)} async-done(((bf16[32,2,256]{2,1,0:T(2,128)(2,1)}), bf16[32,2,256]{2,1,0:T(2,128)(2,1)S(1)}, u32[]{:S(2)}, u32[]{:S(2)}) %all-to-all-start) | async-done | bytes 32800 | tf_op jit(solution)/shard_map/all_to_all | solution.py:175
  24.1 0.2 reshape.159
  24.4 2.1 %gather_fusion = bf16[512,2,16]{2,1,0:T(2,128)(2,1)S(1)} fusion(bf16[512,2,16]{2,1,0:T(2,128)(2,1)S(1)} %reshape.159, s32[1024]{0:T(1024)S(1)} %pad_clamp_fusion), kind=kCustom, calls=%fused_computation | custom fusion | bytes 67584 | tf_op jit(solution)/shard_map/gather | solution.py:178
  26.5 0.3 reshape.160
  26.8 16.6 %all_to_all.20 = bf16[8,2,1024]{2,1,0:T(2,128)(2,1)S(1)} all-to-all(bf16[8,2,1024]{2,1,0:T(2,128)(2,1)S(1)} %reshape.160), channel_id=1, replica_groups=mesh['row'=32,'src'=8] {'src'}, dimensions={0} | all-to-all | bytes 65536 | tf_op jit(solution)/shard_map/all_to_all | solution.py:180
  43.4 0.2 reshape.161
  43.6 0.2 copy.15
  43.7 0.1 copy.13.panel_ref
  43.8 0.0 copy-done.1
  43.9 0.0 copy-start
  43.9 2.2 %copy-done = bf16[2,512,32,64]{1,3,2,0:T(8,128)(2,1)S(1)} copy-done((bf16[2,512,32,64]{1,3,2,0:T(8,128)(2,1)S(1)}, bf16[2,512,32,64]{1,3,2,0:T(8,128)(2,1)}, u32[]{:S(2)}) %copy-start) | copy-done | bytes 4194328
  46.0 69.7 %predict.1 = (f32[64,256]{1,0:T(8,128)S(1)}, f32[64,256]{1,0:T(8,128)S(1)}) custom-call(f32[2]{0:T(128)S(1)} %copy-done.1, bf16[64,256]{1,0:T(8,128)(2,1)S(1)} %copy.13.panel_ref, bf16[2,2048,512]{2,1,0:T(8,128)(2,1)S(1)} %bitcast.17), custom_call_target="tpu_custom_call" | custom-call | tf_op jit(solution)/shard_map/predict/pallas_call | solution.py:189
  115.7 0.7 reshape.147
  116.4 0.7 reshape.148
  (2 shorter events, 0.0 us)
Async XLA Ops:
  0.6 16.4 %copy-start.2 = (s32[512]{0:T(512)S(1)}, s32[512]{0:T(512)}, u32[]{:S(2)}) copy-start(s32[512]{0:T(512)} %param.5) | copy-start | bytes 6148
  0.6 43.2 %copy-start.1 = (f32[2]{0:T(128)S(1)}, f32[2]{0:T(128)}, u32[]{:S(2)}) copy-start(f32[2]{0:T(128)} %wave_ref.1) | copy-start | bytes 28
  7.8 16.4 %all-to-all-start = ((bf16[32,2,256]{2,1,0:T(2,128)(2,1)}), bf16[32,2,256]{2,1,0:T(2,128)(2,1)S(1)}, u32[]{:S(2)}, u32[]{:S(2)}) async-start(bf16[32,2,256]{2,1,0:T(2,128)(2,1)} %reshape.158), calls=%async_computation | async-start | bytes 65536 | tf_op jit(solution)/shard_map/all_to_all | solution.py:175
  43.9 2.2 %copy-start = (bf16[2,512,32,64]{1,3,2,0:T(8,128)(2,1)S(1)}, bf16[2,512,32,64]{1,3,2,0:T(8,128)(2,1)}, u32[]{:S(2)}) copy-start(bf16[2,512,32,64]{1,3,2,0:T(8,128)(2,1)} %param.6) | copy-start | bytes 12582916

commit v2 on v0

v2 whole, which is shorter than its diff:
```python
import contextlib
import functools

import jax
import jax.numpy as jnp
from jax import lax
from jax.experimental import pallas as pl
from jax.experimental.pallas import tpu as pltpu
from jax.sharding import PartitionSpec as P

FREQ = 61
ITERS = 3
HALVES = 2
SIDES = (4, 4)
MESH = pl.DeviceIdType.MESH
F32, BF16 = jnp.float32, jnp.bfloat16


def dft_kernel(samples):
    ticks = jnp.arange(samples, dtype=jnp.int32)
    moment = ticks.astype(jnp.float32)
    ramp_len = samples // 8
    rising = 0.5 - 0.5 * jnp.cos(jnp.pi * (moment + 0.5) / ramp_len)
    falling = 0.5 - 0.5 * jnp.cos(jnp.pi * (samples - moment - 0.5) / ramp_len)
    taper = jnp.where(
        ticks < ramp_len,
        rising,
        jnp.where(ticks >= samples - ramp_len, falling, jnp.ones_like(rising)),
    )
    wrapped = ticks * FREQ % samples
    angles = 2.0 * jnp.pi / samples * wrapped.astype(jnp.float32)
    factor = 1.0 / jnp.sqrt(jnp.float32(samples))
    table = (taper * jnp.cos(angles) * factor, -taper * jnp.sin(angles) * factor)
    return [part.astype(BF16).astype(F32).reshape(1, samples) for part in table]


def stage(name):
    return contextlib.nullcontext()


def log2(n):
    assert n & (n - 1) == 0, n
    return n.bit_length() - 1


def iota(shape, axis):
    return lax.broadcasted_iota(jnp.int32, shape, axis)


def predict(
    sizes, wave_ref, real_ref, imag_ref, source_ref, traces_ref, data_ref, mult_ref, prim_ref,
    traces, staged, estimate, spread, place, chosen, spectra, arrived, packed, pieces,
    base, gathered, whole, sent, came,
    tr_sem, load_sem, a_send, a_recv, b_send, b_recv,
    ag_send, ag_recv, ag_beside, rs_send, rs_recv,
):
    n_row, n_src, rows, shot_local, sides = sizes
    n_zed = n_src // 2
    row, src = lax.axis_index("row"), lax.axis_index("src")
    zed, core = lax.div(src, 2), lax.rem(src, 2)
    block_rows = rows * n_src
    group = block_rows // n_row
    depth = n_row * rows
    shots = n_src * shot_local
    per_half = shots // HALVES
    chunks, chunk = traces.shape[0], traces.shape[1]
    packs = rows // group

    def trace_copy(k):
        at = pl.multiple_of(k * chunk, chunk)
        return pltpu.make_async_copy(traces_ref.at[pl.ds(at, chunk)], traces.at[k], tr_sem.at[k])

    ahead = 4
    for k in range(ahead):
        trace_copy(k).start()

    barrier = pltpu.get_barrier_semaphore()

    @pl.loop(1, n_row)
    def _(k):
        pl.semaphore_signal(barrier, inc=1, device_id=(lax.rem(row + k, n_row), src), device_id_type=MESH)

    @pl.loop(1, n_src)
    def _(k):
        pl.semaphore_signal(barrier, inc=1, device_id=(row, lax.rem(src + k, n_src)), device_id_type=MESH)

    load = pltpu.make_async_copy(data_ref, staged, load_sem)

    lanes = 8 * shot_local
    from_lane, to_lane = iota((2 * lanes, lanes), 0), iota((2 * lanes, lanes), 1)
    same = (from_lane >> log2(lanes) == (to_lane >> log2(shot_local) & 1)) & (
        (from_lane ^ to_lane) & (shot_local - 1) == 0
    )
    spread[...] = jnp.where(same, 1.0, 0.0).astype(BF16)
    table_row = iota((16, real_ref.shape[1]), 0)
    table = jnp.where(table_row == 0, real_ref[...], jnp.where(table_row == 1, imag_ref[...], 0.0)).astype(BF16)
    own_lanes = iota((8, lanes), 1) >> log2(shot_local) == iota((8, lanes), 0)

    @pl.loop(0, chunks)
    def _(k):
        with stage("trace wait"):
            trace_copy(k).wait()

        @pl.when(k + ahead < chunks)
        def _():
            trace_copy(k + ahead).start()

        @pl.when(k + ahead == chunks)
        def _():
            load.start()

        spectrum = lax.dot_general(
            table, traces[k], (((1,), (1,)), ((), ())), preferred_element_type=F32
        )
        parts = []
        for c in range(2):
            pieces_of = [
                jnp.where(own_lanes, jnp.broadcast_to(spectrum[c : c + 1, g : g + lanes], (8, lanes)), 0.0)
                for g in range(0, chunk, lanes)
            ]
            parts.append(jnp.concatenate(pieces_of, axis=0).astype(BF16))
        block = jnp.dot(jnp.concatenate(parts, axis=1), spread[...], preferred_element_type=F32)
        block = block.astype(BF16).reshape(-1, group, lanes)
        groups = block.shape[0]
        spectra[pl.ds(k * groups, groups)] = block

    with stage("barrier"):
        pl.semaphore_wait(barrier, n_row - 1 + n_src - 1)

    def to_row(k):
        target = lax.rem(row + k, n_row)
        return pltpu.make_async_remote_copy(
            src_ref=spectra.at[target],
            dst_ref=arrived.at[row],
            send_sem=a_send,
            recv_sem=a_recv,
            device_id=(target, src),
            device_id_type=MESH,
        )

    @pl.loop(1, n_row)
    def _(k):
        to_row(k).start()

    arrived[row] = spectra[row]

    where = source_ref[...]
    located = (where >> log2(block_rows)) * group + (where & (group - 1))
    width = 256
    for at in range(0, block_rows, width):
        hit = iota((block_rows, width), 0) == jnp.broadcast_to(located[:, at : at + width], (block_rows, width))
        turned = jnp.where(hit, 1.0, 0.0).astype(BF16).T
        for u in range(0, width, group):
            device, pack = (at + u) // rows, (at + u) % rows // group
            to = (pack * n_src + device) * group
            chosen[to : to + group, :] = turned[u : u + group, :]

    from_lane, to_lane = iota((n_src * lanes, 2 * shots), 0), iota((n_src * lanes, 2 * shots), 1)
    shot = (from_lane >> log2(lanes)) * shot_local + (from_lane & (shot_local - 1))
    imag = from_lane >> log2(shot_local) & 1
    goal = (shot >> log2(per_half)) * (2 * per_half) + imag * per_half + (shot & (per_half - 1))
    place[...] = jnp.where(goal == to_lane, 1.0, 0.0).astype(BF16)

    def wait_for(ref, count, sem):
        pltpu.make_async_copy(ref.at[pl.ds(0, count)], ref.at[pl.ds(0, count)], sem).wait()

    with stage("row wait"):
        wait_for(arrived, n_row - 1, a_recv)
    ordered = jnp.dot(
        chosen[...], arrived[...].reshape(block_rows, lanes), preferred_element_type=F32
    ).reshape(packs, n_src * group, lanes)
    own_pack = iota((n_src * group, lanes), 1) >> log2(2 * shot_local)
    joined = jnp.zeros((n_src * group, lanes), F32)
    for p in range(packs):
        joined = jnp.where(own_pack == p, ordered[p], joined)
    packed[...] = joined.astype(BF16).reshape(n_src, group, lanes)

    def to_src(k):
        target = lax.rem(src + k, n_src)
        return pltpu.make_async_remote_copy(
            src_ref=packed.at[target],
            dst_ref=pieces.at[src],
            send_sem=b_send,
            recv_sem=b_recv,
            device_id=(row, target),
            device_id_type=MESH,
        )

    @pl.loop(1, n_src)
    def _(k):
        to_src(k).start()

    pieces[src] = packed[src]

    load.wait()

    with stage("src wait"):
        wait_for(pieces, n_src - 1, b_recv)
    lane_pack = iota((group, lanes), 1) >> log2(2 * shot_local)
    left = []
    for s in range(n_src):
        piece = pieces[s].astype(F32)
        left.append(
            jnp.concatenate([jnp.where(lane_pack == p, piece, 0.0) for p in range(packs)], axis=0).astype(BF16)
        )
    panel = jnp.dot(jnp.concatenate(left, axis=1), place[...], preferred_element_type=F32)

    side_x, side_y = sides
    along_x, along_y, along_z = row // (2 * side_y), row // 2 % side_y, row % 2
    beside = row + 1 - 2 * along_z

    def in_plane(k):
        to_x, to_y = lax.rem(along_x + k // side_y, side_x), lax.rem(along_y + k % side_y, side_y)
        return (to_x * side_y + to_y) * 2 + along_z

    def send_block(it, h, slot, target, sem):
        return pltpu.make_async_remote_copy(
            src_ref=gathered.at[it, h, slot],
            dst_ref=gathered.at[it, h, slot],
            send_sem=ag_send.at[it, h],
            recv_sem=sem.at[it, h],
            device_id=(target, src),
            device_id_type=MESH,
        )

    def spread_block(it, h, slot):
        @pl.loop(1, side_x * side_y)
        def _(k):
            send_block(it, h, slot, in_plane(k), ag_recv).start()

    def share(it, h, value):
        gathered[it, h, row] = value.astype(BF16)
        send_block(it, h, row, beside, ag_beside).start()
        spread_block(it, h, row)

    def relay(it, h):
        with stage("relay"):
            send_block(it, h, beside, beside, ag_beside).wait_recv()
        spread_block(it, h, beside)

    width = 2 * per_half
    for h in range(HALVES):
        base[h] = panel[:, h * width : (h + 1) * width]
        share(0, h, base[h])
    for h in range(HALVES):
        relay(0, h)

    def to_owner(it, h, chip, c):
        return pltpu.make_async_remote_copy(
            src_ref=sent.at[it, h, chip, c],
            dst_ref=came.at[it, h, src],
            send_sem=rs_send.at[it, h],
            recv_sem=rs_recv.at[it, h],
            device_id=(row, chip * 2 + c),
            device_id_type=MESH,
        )

    sign = jnp.where(iota((1, width), 1) < per_half, -1.0, 1.0)

    def crossed(v):
        return pltpu.roll(v, per_half, 1) * sign

    def multiply(it, h):
        with stage("gather wait"):
            wait_for(gathered.at[it, h], n_row - 2, ag_recv.at[it, h])
        with stage("multiply"):
            estimate[h] = gathered.at[it, h].reshape(depth, width)[...].T
            for near in range(2):
                pair = lax.rem(zed // 2 + 1 + near, 2)
                columns = pl.ds(pl.multiple_of(pair * 4 * rows, 4 * rows), 4 * rows)
                real_terms, imag_terms = (
                    jnp.dot(estimate[h], staged[c, :, columns], preferred_element_type=F32) for c in range(2)
                )
                real = real_terms[:per_half] - imag_terms[per_half:]
                imag = real_terms[per_half:] + imag_terms[:per_half]
                both = jnp.concatenate([real, imag], axis=0).T.reshape(2, 2, rows, width)
                sent[it, h, pl.ds(pair * 2, 2)] = both.astype(BF16)
                if near:
                    for c in range(2):
                        to_owner(it, h, zed + 1 - 2 * lax.rem(zed, 2), c).start()
                    to_owner(it, h, zed, 1 - core).start()
                    whole[h] = both
                else:
                    for n in range(2):
                        for c in range(2):
                            to_owner(it, h, pair * 2 + n, c).start()

    wave_real, wave_imag = wave_ref[0], wave_ref[1]

    def finish(it, h):
        with stage("sum wait"):
            wait_for(came.at[it, h], n_src - 1, rs_recv.at[it, h])
        total = whole[h, lax.rem(zed, 2), core]
        for k in range(1, n_src):
            total = total + came[it, h, lax.rem(src + k, n_src)].astype(F32)
        return total, base[h] - (wave_real * total + wave_imag * crossed(total))

    @pl.loop(0, ITERS - 1)
    def _(it):
        for h in range(HALVES):
            multiply(it, h)
            if h:
                relay(it + 1, h - 1)
            else:

                @pl.when(it > 0)
                def _():
                    relay(it, HALVES - 1)

            share(it + 1, h, finish(it, h)[1])

    multiply(ITERS - 1, 0)
    relay(ITERS - 1, 1)
    multiply(ITERS - 1, 1)
    for h in range(HALVES):
        total, primary = finish(ITERS - 1, h)
        for c in range(2):
            to = c * shots + h * per_half
            mult_ref[:, to : to + per_half] = total[:, c * per_half : (c + 1) * per_half]
            prim_ref[:, to : to + per_half] = primary[:, c * per_half : (c + 1) * per_half]

    wait_for(spectra, n_row - 1, a_send)
    wait_for(packed, n_src - 1, b_send)

    @pl.loop(0, ITERS)
    def _(it):
        for h in range(HALVES):
            wait_for(gathered.at[it, h], n_row - 1, ag_send.at[it, h])
            wait_for(came.at[it, h], n_src - 1, rs_send.at[it, h])


def body(traces, row_source, slice_data, wavelet_inverse):
    block_rows, shot_local, samples = traces.shape
    n_row, n_src = lax.axis_size("row"), lax.axis_size("src")
    n_zed = n_src // 2
    rows = block_rows // n_src
    group = block_rows // n_row
    shots = n_src * shot_local
    depth = n_row * rows
    width = 2 * shots // HALVES
    lanes = 8 * shot_local
    chunk = 1024
    chunks = block_rows * shot_local // chunk
    real_table, imag_table = dft_kernel(samples)
    data = jnp.transpose(slice_data, (0, 2, 3, 1)).reshape(2, depth, block_rows)
    block = jax.ShapeDtypeStruct((rows, 2 * shots), F32)
    vmem, sems = pltpu.VMEM, pltpu.SemaphoreType.DMA
    multiples, primaries = pl.pallas_call(
        functools.partial(predict, (n_row, n_src, rows, shot_local, SIDES)),
        out_shape=(block, block),
        in_specs=[
            pl.BlockSpec(memory_space=pltpu.SMEM),
            pl.BlockSpec(memory_space=pltpu.VMEM),
            pl.BlockSpec(memory_space=pltpu.VMEM),
            pl.BlockSpec(memory_space=pltpu.VMEM),
            pl.BlockSpec(memory_space=pltpu.HBM),
            pl.BlockSpec(memory_space=pltpu.HBM),
        ],
        out_specs=(pl.BlockSpec(memory_space=pltpu.VMEM),) * 2,
        scratch_shapes=[
            vmem((chunks, chunk, samples), BF16),
            vmem((2, depth, block_rows), BF16),
            vmem((HALVES, width, depth), BF16),
            vmem((2 * lanes, lanes), BF16),
            vmem((n_src * lanes, 2 * shots), BF16),
            vmem((block_rows, block_rows), BF16),
            vmem((n_row, group, lanes), BF16),
            vmem((n_row, group, lanes), BF16),
            vmem((n_src, group, lanes), BF16),
            vmem((n_src, group, lanes), BF16),
            vmem((HALVES, rows, width), F32),
            vmem((ITERS, HALVES, n_row, rows, width), BF16),
            vmem((HALVES, 2, 2, rows, width), F32),
            vmem((ITERS, HALVES, n_zed, 2, rows, width), BF16),
            vmem((ITERS, HALVES, n_src, rows, width), BF16),
            sems((chunks,)),
            sems,
            sems,
            sems,
            sems,
            sems,
            sems((ITERS, HALVES)),
            sems((ITERS, HALVES)),
            sems((ITERS, HALVES)),
            sems((ITERS, HALVES)),
            sems((ITERS, HALVES)),
        ],
        compiler_params=pltpu.CompilerParams(
            collective_id=0, has_side_effects=True, vmem_limit_bytes=52 << 20
        ),
        name="predict",
    )(
        wavelet_inverse,
        real_table,
        imag_table,
        row_source.reshape(1, block_rows),
        traces.reshape(block_rows * shot_local, samples),
        data,
    )
    shape = (rows, 2, shots)
    return multiples.reshape(shape), primaries.reshape(shape)


def solution(mesh):
    in_specs = (P("row", "src", None), P("row"), P(None, "row", None, "src"), P())
    out_specs = (P(("row", "src"), None, None), P(("row", "src"), None, None))
    return jax.shard_map(body, mesh=mesh, in_specs=in_specs, out_specs=out_specs, check_vma=False)
```

time: 754 us -> 86.2 us (0.11)
  waiting for transfers between devices: 674 us -> 0 us
  Pallas kernels: 0 us -> 82.7 us
  blocking collectives: 16.6 us -> 0 us
  matrix products: 16 us -> 0 us
  between operations: 14.4 us -> 0.65 us
  local copies, waits for them, and re-layouts: 13.5 us -> 2.66 us
  starting transfers between devices: 9.46 us -> 0 us
  other arithmetic: 9.38 us -> 0.11 us
    all_gather x3 -> x0, waiting for transfers between devices: 383 us -> none  [body(): shard_rows = lax.all_gather(estimate, 'row', axis=0, tiled=True)]
    psum x3 -> x0, waiting for transfers between devices: 285 us -> none  [body(): summed = lax.psum(combine_parts(real_terms, imag_terms, shot_count), 'src')]
    pallas_call x0 -> x1, Pallas kernels: none -> 82.7 us  [body(): pl.pallas_call(functools.partial(predict, (n_row, n_src, rows, shot_local...]
    all_to_all x1 -> x0, blocking collectives: 16.6 us -> none  [body(): lax.all_to_all(ordered, 'src', split_axis=0, concat_axis=2, tiled=True)]
    dot_general x7 -> x0, matrix products: 16 us -> none  [the longest x3 8.18 us: body(): imag_terms = jnp.dot(imag_data, stacked, preferred_element_type=jnp.float32)]
    all_to_all x1 -> x0, starting transfers between devices: 9.21 us -> none  [body(): lax.all_to_all(spectra, 'row', split_axis=0, concat_axis=0, tiled=True)]
  transfers between devices with their start and end apart: 7 -> 0, of which waited for: 7 -> 0; matrix products, arithmetic and copies ran while one was open for 1% -> 0% of each run, Pallas kernels for 0% -> 0%
where the time goes in v2:
time: 86.2 us; the launch traced here: 86.1 us
  Pallas kernels  82.7 us (96%)
  local copies, waits for them, and re-layouts  2.66 us (3%)
    pallas_call x1, Pallas kernels, body(): pl.pallas_call(functools.partial(predict, (n_row, n_src, rows, shot_local...  82.7 us

profile of v2, /device:TPU:1, one launch (start us, length us, event | category | flops | bytes accessed | tf_op | source)
XLA Modules:
  0.0 86.1 jit_solution(4183329318748115111)
XLA Ops:
  0.6 0.1 convert_convert_fusion
  0.7 0.0 copy-start
  0.8 0.7 copy-done
  1.4 0.0 copy-start.1
  1.4 0.7 copy-done.1
  2.1 82.7 %predict.1 = (f32[64,256]{1,0:T(8,128)S(1)}, f32[64,256]{1,0:T(8,128)S(1)}) custom-call(f32[2]{0:T(128)S(1)} %copy-done.1, f32[1,512]{1,0:T(1,128)S(1)} %get-tuple-element.7.real_ref, f32[1,512]{1,0:T(1,128)S(1)} %get-tuple-element.6.imag_ref, s32[1,512]{1,0:T(1,128)S(1)} %bitcast.5, bf16[8192,512]{1,0:T(8,128)(2,1)} %bitcast.6, bf16[2,2048,512]{2,1,0:T(8,128)(2,1)} %bitcast.7), custom_call_target="tpu_custom_call" | custom-call | tf_op jit(solution)/shard_map/predict/pallas_call | solution.py:348
  84.7 0.7 reshape.158
  85.4 0.7 reshape.159
Async XLA Ops:
  0.7 0.7 copy-start
  1.4 0.7 copy-start.1

commit v3 on v2

--- a/solution.py
+++ b/solution.py
@@ -11,13 +11,14 @@
 FREQ = 61
 ITERS = 3
 HALVES = 2
+NEAR = 4
 SIDES = (4, 4)
 MESH = pl.DeviceIdType.MESH
 F32, BF16 = jnp.float32, jnp.bfloat16
 
 
-def dft_kernel(samples):
-    ticks = jnp.arange(samples, dtype=jnp.int32)
+def dft_kernel(samples, lines):
+    ticks, line = iota((lines, samples), 1), iota((lines, samples), 0)
     moment = ticks.astype(jnp.float32)
     ramp_len = samples // 8
     rising = 0.5 - 0.5 * jnp.cos(jnp.pi * (moment + 0.5) / ramp_len)
@@ -30,8 +31,8 @@
     wrapped = ticks * FREQ % samples
     angles = 2.0 * jnp.pi / samples * wrapped.astype(jnp.float32)
     factor = 1.0 / jnp.sqrt(jnp.float32(samples))
-    table = (taper * jnp.cos(angles) * factor, -taper * jnp.sin(angles) * factor)
-    return [part.astype(BF16).astype(F32).reshape(1, samples) for part in table]
+    table = jnp.where(line == 0, taper * jnp.cos(angles) * factor, -taper * jnp.sin(angles) * factor)
+    return table.astype(BF16).astype(F32)
 
 
 def stage(name):
@@ -48,11 +49,11 @@
 
 
 def predict(
-    sizes, wave_ref, real_ref, imag_ref, source_ref, traces_ref, data_ref, mult_ref, prim_ref,
-    traces, staged, estimate, spread, place, chosen, spectra, arrived, packed, pieces,
+    sizes, small_ref, traces_ref, data_ref, mult_ref, prim_ref,
+    traces, staged, estimate, first, spread, place, chosen, spectra, arrived, packed, pieces,
     base, gathered, whole, sent, came,
     tr_sem, load_sem, a_send, a_recv, b_send, b_recv,
-    ag_send, ag_recv, ag_beside, rs_send, rs_recv,
+    ag_send, ag_recv, ag_other, ag_beside, rs_send, rs_recv,
 ):
     n_row, n_src, rows, shot_local, sides = sizes
     n_zed = n_src // 2
@@ -67,8 +68,7 @@
     packs = rows // group
 
     def trace_copy(k):
-        at = pl.multiple_of(k * chunk, chunk)
-        return pltpu.make_async_copy(traces_ref.at[pl.ds(at, chunk)], traces.at[k], tr_sem.at[k])
+        return pltpu.make_async_copy(traces_ref.at[pl.ds(k * chunk, chunk)], traces.at[k], tr_sem.at[k])
 
     ahead = 4
     for k in range(ahead):
@@ -84,7 +84,9 @@
     def _(k):
         pl.semaphore_signal(barrier, inc=1, device_id=(row, lax.rem(src + k, n_src)), device_id_type=MESH)
 
-    load = pltpu.make_async_copy(data_ref, staged, load_sem)
+    loads = [
+        pltpu.make_async_copy(data_ref.at[c, :, z], staged.at[c, z], load_sem.at[c, z]) for c in range(2) for z in range(2)
+    ]
 
     lanes = 8 * shot_local
     from_lane, to_lane = iota((2 * lanes, lanes), 0), iota((2 * lanes, lanes), 1)
@@ -92,22 +94,20 @@
         (from_lane ^ to_lane) & (shot_local - 1) == 0
     )
     spread[...] = jnp.where(same, 1.0, 0.0).astype(BF16)
-    table_row = iota((16, real_ref.shape[1]), 0)
-    table = jnp.where(table_row == 0, real_ref[...], jnp.where(table_row == 1, imag_ref[...], 0.0)).astype(BF16)
+    samples = small_ref.shape[1]
+    table_row = iota((16, samples), 0)
+    table = jnp.where(table_row == 0, small_ref[0:1], jnp.where(table_row == 1, small_ref[1:2], 0.0)).astype(BF16)
     own_lanes = iota((8, lanes), 1) >> log2(shot_local) == iota((8, lanes), 0)
 
-    @pl.loop(0, chunks)
-    def _(k):
+    for k in range(chunks):
         with stage("trace wait"):
             trace_copy(k).wait()
 
-        @pl.when(k + ahead < chunks)
-        def _():
+        if k + ahead < chunks:
             trace_copy(k + ahead).start()
-
-        @pl.when(k + ahead == chunks)
-        def _():
-            load.start()
+        if k + ahead == chunks:
+            for load in loads:
+                load.start()
 
         spectrum = lax.dot_general(
             table, traces[k], (((1,), (1,)), ((), ())), preferred_element_type=F32
@@ -122,7 +122,7 @@
         block = jnp.dot(jnp.concatenate(parts, axis=1), spread[...], preferred_element_type=F32)
         block = block.astype(BF16).reshape(-1, group, lanes)
         groups = block.shape[0]
-        spectra[pl.ds(k * groups, groups)] = block
+        spectra[k * groups : (k + 1) * groups] = block
 
     with stage("barrier"):
         pl.semaphore_wait(barrier, n_row - 1 + n_src - 1)
@@ -144,7 +144,7 @@
 
     arrived[row] = spectra[row]
 
-    where = source_ref[...]
+    where = small_ref[2:3].astype(jnp.int32)
     located = (where >> log2(block_rows)) * group + (where & (group - 1))
     width = 256
     for at in range(0, block_rows, width):
@@ -192,7 +192,8 @@
 
     pieces[src] = packed[src]
 
-    load.wait()
+    for load in loads:
+        load.wait()
 
     with stage("src wait"):
         wait_for(pieces, n_src - 1, b_recv)
@@ -207,43 +208,52 @@
 
     side_x, side_y = sides
     along_x, along_y, along_z = row // (2 * side_y), row // 2 % side_y, row % 2
+    plane = side_x * side_y
     beside = row + 1 - 2 * along_z
-
-    def in_plane(k):
-        to_x, to_y = lax.rem(along_x + k // side_y, side_x), lax.rem(along_y + k % side_y, side_y)
-        return (to_x * side_y + to_y) * 2 + along_z
-
-    def send_block(it, h, slot, target, sem):
+    other_z = 1 - along_z
+    slot = along_z * plane + row // 2
+    slot_beside = other_z * plane + row // 2
+
+    def away(x, y):
+        return min(x, side_x - x) + min(y, side_y - y)
+
+    offsets = [(x, y) for x in range(side_x) for y in range(side_y) if x or y]
+    offsets.sort(key=lambda o: -away(*o))
+    far = [o for o in offsets if away(*o) > NEAR]
+    near = [o for o in offsets if away(*o) <= NEAR]
+
+    def send_block(it, h, which, target, sem):
         return pltpu.make_async_remote_copy(
-            src_ref=gathered.at[it, h, slot],
-            dst_ref=gathered.at[it, h, slot],
+            src_ref=gathered.at[it, h, which],
+            dst_ref=gathered.at[it, h, which],
             send_sem=ag_send.at[it, h],
             recv_sem=sem.at[it, h],
             device_id=(target, src),
             device_id_type=MESH,
         )
 
-    def spread_block(it, h, slot):
-        @pl.loop(1, side_x * side_y)
-        def _(k):
-            send_block(it, h, slot, in_plane(k), ag_recv).start()
+    def send_over(it, h, which, chips, to_z, sem):
+        for x, y in chips:
+            to_x, to_y = lax.rem(along_x + x, side_x), lax.rem(along_y + y, side_y)
+            send_block(it, h, which, (to_x * side_y + to_y) * 2 + to_z, sem).start()
 
     def share(it, h, value):
-        gathered[it, h, row] = value.astype(BF16)
-        send_block(it, h, row, beside, ag_beside).start()
-        spread_block(it, h, row)
+        gathered[it, h, slot] = value.astype(BF16)
+        send_block(it, h, slot, beside, ag_beside).start()
+        send_over(it, h, slot, far, other_z, ag_other)
+        send_over(it, h, slot, offsets, along_z, ag_recv)
 
     def relay(it, h):
         with stage("relay"):
-            send_block(it, h, beside, beside, ag_beside).wait_recv()
-        spread_block(it, h, beside)
+            send_block(it, h, slot_beside, beside, ag_beside).wait_recv()
+        send_over(it, h, slot_beside, near, along_z, ag_other)
 
     width = 2 * per_half
     for h in range(HALVES):
         base[h] = panel[:, h * width : (h + 1) * width]
         share(0, h, base[h])
-    for h in range(HALVES):
-        relay(0, h)
+        if h == 0:
+            relay(0, 0)
 
     def to_owner(it, h, chip, c):
         return pltpu.make_async_remote_copy(
@@ -261,31 +271,49 @@
         return pltpu.roll(v, per_half, 1) * sign
 
     def multiply(it, h):
+        def terms_of(z, pair):
+            columns = pl.ds(pl.multiple_of(pair * 4 * rows, 4 * rows), 4 * rows)
+            real_terms, imag_terms = (
+                jnp.dot(
+                    estimate[h],
+                    staged.at[c, z].reshape(depth // 2, block_rows)[:, columns],
+                    preferred_element_type=F32,
+                )
+                for c in range(2)
+            )
+            real = real_terms[:per_half] - imag_terms[per_half:]
+            imag = real_terms[per_half:] + imag_terms[:per_half]
+            return jnp.concatenate([real, imag], axis=0)
+
+        def turn(z):
+            at = pl.multiple_of(z * plane, plane)
+            estimate[h] = gathered.at[it, h, pl.ds(at, plane)].reshape(depth // 2, width)[...].T
+
+        pairs = [lax.rem(zed // 2 + 1 + n, 2) for n in range(2)]
+        with stage("plane wait"):
+            wait_for(gathered.at[it, h], plane - 1, ag_recv.at[it, h])
+        with stage("multiply plane"):
+            turn(along_z)
+            for n in range(2):
+                first[n] = terms_of(along_z, pairs[n])
         with stage("gather wait"):
-            wait_for(gathered.at[it, h], n_row - 2, ag_recv.at[it, h])
+            wait_for(gathered.at[it, h], plane - 1, ag_other.at[it, h])
         with stage("multiply"):
-            estimate[h] = gathered.at[it, h].reshape(depth, width)[...].T
-            for near in range(2):
-                pair = lax.rem(zed // 2 + 1 + near, 2)
-                columns = pl.ds(pl.multiple_of(pair * 4 * rows, 4 * rows), 4 * rows)
-                real_terms, imag_terms = (
-                    jnp.dot(estimate[h], staged[c, :, columns], preferred_element_type=F32) for c in range(2)
-                )
-                real = real_terms[:per_half] - imag_terms[per_half:]
-                imag = real_terms[per_half:] + imag_terms[:per_half]
-                both = jnp.concatenate([real, imag], axis=0).T.reshape(2, 2, rows, width)
-                sent[it, h, pl.ds(pair * 2, 2)] = both.astype(BF16)
-                if near:
+            turn(other_z)
+            for n, pair in enumerate(pairs):
+                both = first[n] + terms_of(other_z, pair)
+                sent[it, h, pl.ds(pair * 2, 2)] = both.astype(BF16).T.reshape(2, 2, rows, width)
+                if n:
                     for c in range(2):
                         to_owner(it, h, zed + 1 - 2 * lax.rem(zed, 2), c).start()
                     to_owner(it, h, zed, 1 - core).start()
-                    whole[h] = both
+                    whole[h] = both.T.reshape(2, 2, rows, width)
                 else:
-                    for n in range(2):
+                    for chip in range(2):
                         for c in range(2):
-                            to_owner(it, h, pair * 2 + n, c).start()
-
-    wave_real, wave_imag = wave_ref[0], wave_ref[1]
+                            to_owner(it, h, pair * 2 + lax.rem(zed + chip, 2), c).start()
+
+    wave_real, wave_imag = small_ref[3:4, :width], small_ref[4:5, :width]
 
     def finish(it, h):
         with stage("sum wait"):
@@ -299,14 +327,7 @@
     def _(it):
         for h in range(HALVES):
             multiply(it, h)
-            if h:
-                relay(it + 1, h - 1)
-            else:
-
-                @pl.when(it > 0)
-                def _():
-                    relay(it, HALVES - 1)
-
+            relay(it + h, 1 - h)
             share(it + 1, h, finish(it, h)[1])
 
     multiply(ITERS - 1, 0)
@@ -341,17 +362,18 @@
     lanes = 8 * shot_local
     chunk = 1024
     chunks = block_rows * shot_local // chunk
-    real_table, imag_table = dft_kernel(samples)
-    data = jnp.transpose(slice_data, (0, 2, 3, 1)).reshape(2, depth, block_rows)
+    lines = 8
+    line = iota((lines, samples), 0)
+    wave = lax.broadcast_in_dim(jnp.pad(wavelet_inverse, (3, lines - 5)), (lines, samples), (0,))
+    source = lax.broadcast_in_dim(row_source.astype(F32), (lines, samples), (1,))
+    small = jnp.where(line == 2, source, jnp.where(line > 2, wave, dft_kernel(samples, lines)))
+    data = jnp.transpose(slice_data, (0, 2, 3, 1)).reshape(2, n_row // 2, 2, rows, block_rows)
     block = jax.ShapeDtypeStruct((rows, 2 * shots), F32)
     vmem, sems = pltpu.VMEM, pltpu.SemaphoreType.DMA
     multiples, primaries = pl.pallas_call(
         functools.partial(predict, (n_row, n_src, rows, shot_local, SIDES)),
         out_shape=(block, block),
         in_specs=[
-            pl.BlockSpec(memory_space=pltpu.SMEM),
-            pl.BlockSpec(memory_space=pltpu.VMEM),
-            pl.BlockSpec(memory_space=pltpu.VMEM),
             pl.BlockSpec(memory_space=pltpu.VMEM),
             pl.BlockSpec(memory_space=pltpu.HBM),
             pl.BlockSpec(memory_space=pltpu.HBM),
@@ -359,8 +381,9 @@
         out_specs=(pl.BlockSpec(memory_space=pltpu.VMEM),) * 2,
         scratch_shapes=[
             vmem((chunks, chunk, samples), BF16),
-            vmem((2, depth, block_rows), BF16),
-            vmem((HALVES, width, depth), BF16),
+            vmem((2, 2, n_row // 2, rows, block_rows), BF16),
+            vmem((HALVES, width, depth // 2), BF16),
+            vmem((2, width, 4 * rows), F32),
             vmem((2 * lanes, lanes), BF16),
             vmem((n_src * lanes, 2 * shots), BF16),
             vmem((block_rows, block_rows), BF16),
@@ -374,11 +397,12 @@
             vmem((ITERS, HALVES, n_zed, 2, rows, width), BF16),
             vmem((ITERS, HALVES, n_src, rows, width), BF16),
             sems((chunks,)),
+            sems((2, 2)),
             sems,
             sems,
             sems,
             sems,
-            sems,
+            sems((ITERS, HALVES)),
             sems((ITERS, HALVES)),
             sems((ITERS, HALVES)),
             sems((ITERS, HALVES)),
@@ -390,10 +414,7 @@
         ),
         name="predict",
     )(
-        wavelet_inverse,
-        real_table,
-        imag_table,
-        row_source.reshape(1, block_rows),
+        small,
         traces.reshape(block_rows * shot_local, samples),
         data,
     )

time: 86.2 us -> 80.1 us (0.929)
  Pallas kernels: 82.7 us -> 76.4 us
    pallas_call x1, Pallas kernels: 82.7 us -> 76.4 us  [body(): pl.pallas_call(functools.partial(predict, (n_row, n_src, rows, shot_local...]
    unnamed x4 -> x0, local copies, waits for them, and re-layouts: 1.33 us -> none
where the time goes in v3:
time: 80.1 us; the launch traced here: 80 us
  Pallas kernels  76.4 us (95%)
  local copies, waits for them, and re-layouts  2.06 us (3%)
  other arithmetic  0.87 us (1%)
    pallas_call x1, Pallas kernels, body(): pl.pallas_call(functools.partial(predict, (n_row, n_src, rows, shot_local...  76.4 us

profile of v3, /device:TPU:1, one launch (start us, length us, event | category | flops | bytes accessed | tf_op | source)
XLA Modules:
  0.0 80.0 jit_solution(11236691345557590651)
XLA Ops:
  0.6 0.7 pad.4
  1.4 0.7 convert_element_type.18
  2.1 0.1 fusion.8
  2.2 0.1 select_select_fusion.small_ref
  2.3 76.4 %predict.1 = (f32[64,256]{1,0:T(8,128)S(1)}, f32[64,256]{1,0:T(8,128)S(1)}) custom-call(f32[8,512]{1,0:T(8,128)S(1)} %select_select_fusion.small_ref, bf16[8192,512]{1,0:T(8,128)(2,1)} %bitcast.4, bf16[2,16,2,64,512]{4,3,2,1,0:T(8,128)(2,1)} %bitcast.5), custom_call_target="tpu_custom_call" | custom-call | tf_op jit(solution)/shard_map/predict/pallas_call | solution.py:373
  78.6 0.7 reshape.18
  79.3 0.7 reshape.19
  (5 shorter events, 0.0 us)

commit v4 on v3

--- a/solution.py
+++ b/solution.py
@@ -49,7 +49,7 @@
 
 
 def predict(
-    sizes, small_ref, traces_ref, data_ref, mult_ref, prim_ref,
+    sizes, table_ref, small_ref, traces_ref, data_ref, mult_ref, prim_ref,
     traces, staged, estimate, first, spread, place, chosen, spectra, arrived, packed, pieces,
     base, gathered, whole, sent, came,
     tr_sem, load_sem, a_send, a_recv, b_send, b_recv,
@@ -94,9 +94,9 @@
         (from_lane ^ to_lane) & (shot_local - 1) == 0
     )
     spread[...] = jnp.where(same, 1.0, 0.0).astype(BF16)
-    samples = small_ref.shape[1]
+    samples = table_ref.shape[1]
     table_row = iota((16, samples), 0)
-    table = jnp.where(table_row == 0, small_ref[0:1], jnp.where(table_row == 1, small_ref[1:2], 0.0)).astype(BF16)
+    table = jnp.where(table_row == 0, table_ref[0:1], jnp.where(table_row == 1, table_ref[1:2], 0.0)).astype(BF16)
     own_lanes = iota((8, lanes), 1) >> log2(shot_local) == iota((8, lanes), 0)
 
     for k in range(chunks):
@@ -144,7 +144,7 @@
 
     arrived[row] = spectra[row]
 
-    where = small_ref[2:3].astype(jnp.int32)
+    where = small_ref[:, :block_rows].astype(jnp.int32)
     located = (where >> log2(block_rows)) * group + (where & (group - 1))
     width = 256
     for at in range(0, block_rows, width):
@@ -234,7 +234,8 @@
 
     def send_over(it, h, which, chips, to_z, sem):
         for x, y in chips:
-            to_x, to_y = lax.rem(along_x + x, side_x), lax.rem(along_y + y, side_y)
+            to_x = lax.rem(along_x + side_x + x - 2 * core * x + core * side_x, side_x)
+            to_y = lax.rem(along_y + side_y + y - 2 * core * y + core * side_y, side_y)
             send_block(it, h, which, (to_x * side_y + to_y) * 2 + to_z, sem).start()
 
     def share(it, h, value):
@@ -313,7 +314,7 @@
                         for c in range(2):
                             to_owner(it, h, pair * 2 + lax.rem(zed + chip, 2), c).start()
 
-    wave_real, wave_imag = small_ref[3:4, :width], small_ref[4:5, :width]
+    wave_real, wave_imag = small_ref[:, block_rows : block_rows + 1], small_ref[:, block_rows + 1 : block_rows + 2]
 
     def finish(it, h):
         with stage("sum wait"):
@@ -363,10 +364,9 @@
     chunk = 1024
     chunks = block_rows * shot_local // chunk
     lines = 8
-    line = iota((lines, samples), 0)
-    wave = lax.broadcast_in_dim(jnp.pad(wavelet_inverse, (3, lines - 5)), (lines, samples), (0,))
-    source = lax.broadcast_in_dim(row_source.astype(F32), (lines, samples), (1,))
-    small = jnp.where(line == 2, source, jnp.where(line > 2, wave, dft_kernel(samples, lines)))
+    small = jnp.pad(row_source, (0, 128)).astype(F32) + jnp.pad(wavelet_inverse, (block_rows, 126))
+    small = small.reshape(1, -1)
+    table = dft_kernel(samples, lines)
     data = jnp.transpose(slice_data, (0, 2, 3, 1)).reshape(2, n_row // 2, 2, rows, block_rows)
     block = jax.ShapeDtypeStruct((rows, 2 * shots), F32)
     vmem, sems = pltpu.VMEM, pltpu.SemaphoreType.DMA
@@ -374,6 +374,7 @@
         functools.partial(predict, (n_row, n_src, rows, shot_local, SIDES)),
         out_shape=(block, block),
         in_specs=[
+            pl.BlockSpec(memory_space=pltpu.VMEM),
             pl.BlockSpec(memory_space=pltpu.VMEM),
             pl.BlockSpec(memory_space=pltpu.HBM),
             pl.BlockSpec(memory_space=pltpu.HBM),
@@ -414,6 +415,7 @@
         ),
         name="predict",
     )(
+        table,
         small,
         traces.reshape(block_rows * shot_local, samples),
         data,

time: 80.1 us -> 77.9 us (0.973)
  Pallas kernels: 76.4 us -> 74.9 us
    pallas_call x1, Pallas kernels: 76.4 us -> 74.9 us  [body(): pl.pallas_call(functools.partial(predict, (n_row, n_src, rows, shot_local...]
where the time goes in v4:
time: 77.9 us; the launch traced here: 77.8 us
  Pallas kernels  74.9 us (96%)
  local copies, waits for them, and re-layouts  1.33 us (2%)
  other arithmetic  0.88 us (1%)
    pallas_call x1, Pallas kernels, body(): pl.pallas_call(functools.partial(predict, (n_row, n_src, rows, shot_local...  74.9 us

profile of v4, /device:TPU:1, one launch (start us, length us, event | category | flops | bytes accessed | tf_op | source)
XLA Modules:
  0.0 77.8 jit_solution(1404955579728241474)
XLA Ops:
  0.7 0.7 pad_add_fusion
  1.4 0.1 fusion.9
  1.5 0.1 fusion.table_ref
  1.5 74.9 %predict.1 = (f32[64,256]{1,0:T(8,128)S(1)}, f32[64,256]{1,0:T(8,128)S(1)}) custom-call(f32[8,512]{1,0:T(8,128)S(1)} %fusion.table_ref, f32[1,640]{1,0:T(1,128)S(1)} %reshape.19.small_ref, bf16[8192,512]{1,0:T(8,128)(2,1)} %bitcast.4, bf16[2,16,2,64,512]{4,3,2,1,0:T(8,128)(2,1)} %bitcast.5), custom_call_target="tpu_custom_call" | custom-call | tf_op jit(solution)/shard_map/predict/pallas_call | solution.py:373
  76.5 0.7 reshape.22
  77.2 0.7 reshape.23
  (5 shorter events, 0.0 us)

commit v5 on v4

--- a/solution.py
+++ b/solution.py
@@ -74,16 +74,6 @@
     for k in range(ahead):
         trace_copy(k).start()
 
-    barrier = pltpu.get_barrier_semaphore()
-
-    @pl.loop(1, n_row)
-    def _(k):
-        pl.semaphore_signal(barrier, inc=1, device_id=(lax.rem(row + k, n_row), src), device_id_type=MESH)
-
-    @pl.loop(1, n_src)
-    def _(k):
-        pl.semaphore_signal(barrier, inc=1, device_id=(row, lax.rem(src + k, n_src)), device_id_type=MESH)
-
     loads = [
         pltpu.make_async_copy(data_ref.at[c, :, z], staged.at[c, z], load_sem.at[c, z]) for c in range(2) for z in range(2)
     ]
@@ -98,6 +88,16 @@
     table_row = iota((16, samples), 0)
     table = jnp.where(table_row == 0, table_ref[0:1], jnp.where(table_row == 1, table_ref[1:2], 0.0)).astype(BF16)
     own_lanes = iota((8, lanes), 1) >> log2(shot_local) == iota((8, lanes), 0)
+
+    barrier = pltpu.get_barrier_semaphore()
+
+    @pl.loop(1, n_row)
+    def _(k):
+        pl.semaphore_signal(barrier, inc=1, device_id=(lax.rem(row + k, n_row), src), device_id_type=MESH)
+
+    @pl.loop(1, n_src)
+    def _(k):
+        pl.semaphore_signal(barrier, inc=1, device_id=(row, lax.rem(src + k, n_src)), device_id_type=MESH)
 
     for k in range(chunks):
         with stage("trace wait"):

time: 77.9 us -> 77.9 us (level)
  no operation moved by 1% of the time
where the time goes in v5:
time: 77.9 us; the launch traced here: 77.8 us
  Pallas kernels  74.9 us (96%)
  local copies, waits for them, and re-layouts  1.33 us (2%)
  other arithmetic  0.88 us (1%)
    pallas_call x1, Pallas kernels, body(): pl.pallas_call(functools.partial(predict, (n_row, n_src, rows, shot_local...  74.9 us

profile of v5, /device:TPU:1, one launch (start us, length us, event | category | flops | bytes accessed | tf_op | source)
XLA Modules:
  0.0 77.8 jit_solution(10030150258097311180)
XLA Ops:
  0.7 0.7 pad_add_fusion
  1.4 0.1 fusion.9
  1.5 0.1 fusion.table_ref
  1.5 74.9 %predict.1 = (f32[64,256]{1,0:T(8,128)S(1)}, f32[64,256]{1,0:T(8,128)S(1)}) custom-call(f32[8,512]{1,0:T(8,128)S(1)} %fusion.table_ref, f32[1,640]{1,0:T(1,128)S(1)} %reshape.19.small_ref, bf16[8192,512]{1,0:T(8,128)(2,1)} %bitcast.4, bf16[2,16,2,64,512]{4,3,2,1,0:T(8,128)(2,1)} %bitcast.5), custom_call_target="tpu_custom_call" | custom-call | tf_op jit(solution)/shard_map/predict/pallas_call | solution.py:373
  76.5 0.7 reshape.22
  77.2 0.7 reshape.23
  (5 shorter events, 0.0 us)
